TPU v7x, 256 devices: a whole 4x4x8 slice. The times are simulated.
256 devices in a mesh: dst: 32 (over y, z), src: 8 (over x, core).
Axes of the slice: x: 4, y: 4, z: 8, core: 2. Of those that a mesh axis runs over, the one named last changes fastest.
Arguments:
- transitions: bfloat16 [16384, 128, 128], P(('dst', 'src')), may hold values from 0.0009994507 to 1
- row_block: int32 [16384], P(('dst', 'src')), may hold values from -1 to 1023, as said below
- col_block: int32 [16384], P(('dst', 'src')), may hold values from -1 to 1023, as said below
- beta_last: float32 [32, 128, 8, 128], P(None, 'dst', 'src'), may hold values from 0.2 to 2
- emissions: bfloat16 [2, 32, 128, 8, 128], P(None, None, 'dst', 'src'), may hold values from 0.019897461 to 1
- forward: bfloat16 [2, 32, 128, 8, 128], P(None, None, 'dst', 'src'), may hold values from 0.03 to 125, as said below
Outputs:
- counts: bfloat16 [16384, 128, 128], P(('dst', 'src'))
- beta_first: float32 [32, 128, 8, 128], P(None, 'dst', 'src')
- log_norms: float32 [2, 32], replicated
Inputs may be any that keep to these rules, and one draw needn't show every extreme that they name: `row_block`: slots are grouped by device (index dst * 8 + src), 64 to a device. A live slot holds a block whose source block number r has r % 8 equal to the device's src index and whose destination block lies in the device's dst index's own consecutive equal share of blocks; no block appears twice; live slots come first, and empty ones hold -1 in both arrays. One device has all 64 slots live; each device has at least one. `col_block`: same slots as row_block; -1 exactly where row_block is -1. `forward`: Positive.
All inputs are finite; a program needn't handle non-finite values.
Results may differ from a plain program's by a relative error of at most 0.0029.
Values may be sent and summed in bfloat16 or wider, within the bound.
No kernel may reach another device: no remote copies, remote signals or barrier semaphores. Data moves between devices by JAX's collectives and lax.ppermute only.
A program may use at most 64 MiB of HBM per device.

v0:
```python
import jax
import jax.numpy as jnp
from jax import lax
from jax.sharding import PartitionSpec as P

S = 131072
STEPS = 2


def body(transitions, row_block, col_block, beta_last, emissions, forward):
    source_count = lax.axis_size("src")
    seq_count = beta_last.shape[0]
    local_rows = beta_last.shape[1]
    block_size = beta_last.shape[3]
    slot_count = transitions.shape[0]
    column_count = local_rows * source_count
    total_rows = local_rows * lax.axis_size("dst")
    living = row_block >= 0
    live_float = living.astype(jnp.float32)
    row_local = jnp.where(living, row_block // source_count, 0)
    col_local = jnp.where(living, col_block % column_count, 0)
    beta_piece = beta_last[:, :, 0, :]
    count_sum = jnp.zeros((slot_count, block_size, block_size), jnp.float32)
    log_list = []
    for step_index in range(STEPS):
        emitted = emissions[step_index][:, :, 0, :]
        message = (emitted.astype(jnp.float32) * beta_piece).astype(jnp.bfloat16)
        columns = lax.all_gather(message[:, :, None, :], "src", axis=2, tiled=True)
        columns = columns.reshape(seq_count, column_count, block_size)
        alpha_rows = lax.all_gather(forward[step_index], "dst", axis=1, tiled=True)
        alpha_rows = alpha_rows.reshape(seq_count, total_rows, block_size)
        alpha_picked = jnp.take(alpha_rows, row_local, axis=1)
        picked = jnp.take(columns, col_local, axis=1)
        products = jnp.einsum(
            "bcj,cij->cbi", picked, transitions, preferred_element_type=jnp.float32
        )
        products = products * live_float[:, None, None]
        partial_value = jax.ops.segment_sum(products, row_local, num_segments=total_rows)
        raw_sums = lax.psum_scatter(partial_value, "dst", scatter_dimension=0, tiled=True)
        own_alpha = forward[step_index][:, :, 0, :]
        local_term = jnp.einsum(
            "kbr,bkr->b", raw_sums, own_alpha, preferred_element_type=jnp.float32
        )
        scale_now = lax.psum(local_term, ("dst", "src")) / S
        beta_piece = jnp.transpose(raw_sums / scale_now[None, :, None], (1, 0, 2))
        scaled = (columns.astype(jnp.float32) / scale_now[:, None, None]).astype(jnp.bfloat16)
        scaled_picked = jnp.take(scaled, col_local, axis=1)
        count_sum = count_sum + jnp.einsum(
            "bci,bcj->cij", alpha_picked, scaled_picked, preferred_element_type=jnp.float32
        )
        log_list.append(jnp.log(scale_now))
    counts = (count_sum * transitions.astype(jnp.float32) * live_float[:, None, None]).astype(
        jnp.bfloat16
    )
    return (counts, beta_piece[:, :, None, :], jnp.stack(log_list))


def solution(mesh):
    return jax.shard_map(
        body,
        mesh=mesh,
        in_specs=(
            P(("dst", "src"), None, None),
            P(("dst", "src")),
            P(("dst", "src")),
            P(None, "dst", "src", None),
            P(None, None, "dst", "src", None),
            P(None, None, "dst", "src", None),
        ),
        out_specs=(P(("dst", "src"), None, None), P(None, "dst", "src", None), P()),
        check_vma=False,
    )
```

profile of v0, /device:TPU:1, one launch (start us, length us, event | category | flops | bytes accessed | tf_op | source)
XLA Modules:
  0.0 728.8 jit_solution(5440016924613923832)
XLA Ops:
  9.7 15.9 %all_gather.13 = bf16[32,4,8,128]{3,0,1,2:T(8,128)(2,1)S(1)} all-gather(bf16[32,4,1,128]{3,0,1,2:T(8,128)(2,1)S(1)} %fusion.24), channel_id=1, replica_groups=mesh['dst'=32,'src'=8] {'src'}, dimensions={2}, use_global_device_ids=true | all-gather | bytes 294912 | tf_op jit(solution)/shard_map/all_gather | solution.py:28
  25.9 1.4 gather_fusion.1
  27.3 2.3 convolution_multiply_fusion.1
  29.6 1.6 broadcast.28.clone
  31.2 8.0 %scatter_fusion = f32[128,32,128]{2,1,0:T(8,128)} fusion(f32[128,32,128]{2,1,0:T(8,128)} %broadcast.28.clone, s32[64]{0:T(128)S(1)} %get-tuple-element.28, f32[64,32,128]{2,1,0:T(8,128)S(1)} %convolution_multiply_fusion.1), kind=kCustom, calls=%fused_computation.6 | custom fusion | flops 262144 | bytes 3145984 | tf_op jit(solution)/shard_map/scatter-add | solution.py:38
  40.8 213.9 %reduce-scatter.3.cloned.1.call-done = f32[4,32,128]{2,1,0:T(8,128)} async-done(((f32[128,32,128]{2,1,0:T(8,128)}), f32[4,32,128]{2,1,0:T(8,128)}) %reduce-scatter.3.cloned.1.call-update) | async-done | bytes 65552 | tf_op jit(solution)/shard_map/reduce_scatter | solution.py:39
  254.7 1.0 multiply_reduce_fusion.1
  255.7 79.9 %psum.14 = f32[32]{0:T(128)S(1)} all-reduce(f32[32]{0:T(128)S(1)} %multiply_reduce_fusion.1), channel_id=1, replica_groups=mesh['dst'=32,'src'=8] {'dst','src'}, use_global_device_ids=true, to_apply=%region_2.5 | all-reduce | flops 32 | bytes 256 | tf_op jit(solution)/shard_map/psum | solution.py:44
  335.6 0.9 fusion.23
  336.5 12.6 %all-gather.2 = bf16[32,4,1024]{2,0,1:T(8,128)(2,1)S(1)} all-gather(bf16[32,4,128]{2,0,1:T(8,128)(2,1)S(1)} %fusion.23), channel_id=4, replica_groups=mesh['dst'=32,'src'=8] {'src'}, dimensions={2}, use_global_device_ids=true | all-gather | bytes 294912 | tf_op jit(solution)/shard_map/all_gather | solution.py:28
  350.1 1.4 gather_fusion.4
  351.6 2.3 convolution_multiply_fusion
  353.8 1.6 broadcast.28
  355.4 8.0 %scatter_fusion.1 = f32[128,32,128]{2,1,0:T(8,128)} fusion(f32[128,32,128]{2,1,0:T(8,128)} %broadcast.28, s32[64]{0:T(128)S(1)} %copy-done.6, f32[64,32,128]{2,1,0:T(8,128)S(1)} %convolution_multiply_fusion), kind=kCustom, calls=%fused_computation.7 | custom fusion | flops 262144 | bytes 3145984 | tf_op jit(solution)/shard_map/scatter-add | solution.py:38
  363.6 1.9 gather_fusion.3
  365.5 43.8 %all-gather.6.cloned.1.call-done = bf16[1,32,128,1,128]{4,1,3,0,2:T(8,128)(2,1)} async-done(((bf16[1,32,4,1,128]{4,1,3,0,2:T(8,128)(2,1)}), bf16[1,32,128,1,128]{4,1,3,0,2:T(8,128)(2,1)}) %all-gather.6.cloned.1.call-update) | async-done | bytes 1048592 | tf_op jit(solution)/shard_map/all_gather | solution.py:30
  409.3 2.6 gather_fusion
  412.0 1.4 gather_fusion.2
  413.5 216.1 %reduce-scatter.5.cloned.1.call-done = f32[4,32,128]{2,1,0:T(8,128)} async-done(((f32[128,32,128]{2,1,0:T(8,128)}), f32[4,32,128]{2,1,0:T(8,128)}) %reduce-scatter.5.cloned.1.call-update) | async-done | bytes 65552 | tf_op jit(solution)/shard_map/reduce_scatter | solution.py:39
  629.6 1.0 multiply_reduce_fusion
  630.6 4.1 fusion.3
  634.7 79.6 %psum.15 = f32[32]{0:T(128)S(1)} all-reduce(f32[32]{0:T(128)S(1)} %multiply_reduce_fusion), channel_id=1, replica_groups=mesh['dst'=32,'src'=8] {'dst','src'}, use_global_device_ids=true, to_apply=%region_5.8 | all-reduce | flops 32 | bytes 256 | tf_op jit(solution)/shard_map/psum | solution.py:44
  715.2 1.4 gather_fusion.5
  717.2 5.0 multiply_convert_fusion
  (44 shorter events, 7.0 us)
Async XLA Ops:
  7.2 20.2 %copy-start = (bf16[64,128,128]{2,1,0:T(8,128)(2,1)S(1)}, bf16[64,128,128]{2,1,0:T(8,128)(2,1)}, u32[]{:S(2)}) copy-start(bf16[64,128,128]{2,1,0:T(8,128)(2,1)} %param.10) | copy-start | bytes 6291460
  7.2 247.6 %reduce-scatter.3.cloned.1.call-start = ((), (), s32[]{:S(2)}) async-start(), calls=%async_computation.2 | async-start | bytes 2162688 | tf_op jit(solution)/shard_map/reduce_scatter | solution.py:39
  8.1 23.1 %copy-start.5 = (s32[64]{0:T(128)}, s32[64]{0:T(128)S(1)}, u32[]{:S(2)}) copy-start(s32[64]{0:T(128)S(1)} %get-tuple-element.28) | copy-start | bytes 772
  31.2 8.1 %copy-start.4 = (bf16[2,32,4,1,128]{4,2,3,1,0:T(4,128)(2,1)S(1)}, bf16[2,32,4,1,128]{4,2,3,1,0:T(4,128)(2,1)}, u32[]{:S(2)}) copy-start(bf16[2,32,4,1,128]{4,2,3,1,0:T(4,128)(2,1)} %param.15) | copy-start | bytes 196612
  39.3 324.3 %all-gather.8.cloned.1.call-start = ((), (), s32[]{:S(2)}) async-start(), calls=%async_computation.5 | async-start | bytes 1081344 | tf_op jit(solution)/shard_map/all_gather | solution.py:30
  40.0 369.3 %all-gather.6.cloned.1.call-start = ((), (), s32[]{:S(2)}) async-start(), calls=%async_computation.4 | async-start | bytes 1081344 | tf_op jit(solution)/shard_map/all_gather | solution.py:30
  40.8 588.9 %reduce-scatter.5.cloned.1.call-start = ((), (), s32[]{:S(2)}) async-start(), calls=%async_computation.3 | async-start | bytes 2162688 | tf_op jit(solution)/shard_map/reduce_scatter | solution.py:39
  349.4 0.7 copy-start.1
  351.6 3.9 copy-start.6
  630.6 83.8 %copy-start.2 = (bf16[32,32,128]{2,1,0:T(8,128)(2,1)S(1)}, bf16[32,32,128]{2,1,0:T(8,128)(2,1)}, u32[]{:S(2)}) copy-start(bf16[32,32,128]{2,1,0:T(8,128)(2,1)} %copy-done.1) | copy-start | bytes 786436
  630.6 83.9 %copy-start.3 = (f32[4,32,128]{2,1,0:T(8,128)S(1)}, f32[4,32,128]{2,1,0:T(8,128)}, u32[]{:S(2)}) copy-start(f32[4,32,128]{2,1,0:T(8,128)} %reduce-scatter.5.cloned.1.call-done) | copy-start | bytes 196612
Sparse Core Ops, SparseCore 0:
  39.4 215.2 reduce-scatter.2
  257.3 74.8 all-gather.7
  335.4 73.8 all-gather.5
  413.5 216.0 reduce-scatter.4
where the time goes:
time: 730 us; the launch traced here: 729 us
  waiting for transfers between devices  474 us (65%)
  blocking collectives  188 us (26%)
  other arithmetic  21.5 us (3%)
  local copies, waits for them, and re-layouts  17.5 us (2%)
  between operations  13.9 us (2%)
  matrix products  13.7 us (2%)
    reduce_scatter x2, waiting for transfers between devices, body(): lax.psum_scatter(partial_value, 'dst', scatter_dimension=0, tiled=True)  430 us
    psum x2, blocking collectives, body(): scale_now = lax.psum(local_term, ('dst', 'src')) / S  160 us
    all_gather x2, waiting for transfers between devices, body(): alpha_rows = lax.all_gather(forward[step_index], 'dst', axis=1, tiled=True)  43.8 us
    all_gather x2, blocking collectives, body(): columns = lax.all_gather(message[:, :, None, :], 'src', axis=2, tiled=True)  28.5 us
    scatter-add x2, other arithmetic, body(): jax.ops.segment_sum(products, row_local, num_segments=total_rows)  16.1 us
  transfers between devices with their start and end apart: 4, of which 3 were waited for; matrix products, arithmetic and copies ran while one was open for 3% of the time, Pallas kernels for 0%

commit v1 on v0

--- a/solution.py
+++ b/solution.py
@@ -27,7 +27,7 @@
         message = (emitted.astype(jnp.float32) * beta_piece).astype(jnp.bfloat16)
         columns = lax.all_gather(message[:, :, None, :], "src", axis=2, tiled=True)
         columns = columns.reshape(seq_count, column_count, block_size)
-        alpha_rows = lax.all_gather(forward[step_index], "dst", axis=1, tiled=True)
+        alpha_rows = jnp.concatenate(lax.all_gather(forward[step_index], "dst"), axis=1)
         alpha_rows = alpha_rows.reshape(seq_count, total_rows, block_size)
         alpha_picked = jnp.take(alpha_rows, row_local, axis=1)
         picked = jnp.take(columns, col_local, axis=1)

time: 730 us -> 730 us (level)
  no operation moved by 1% of the time
where the time goes in v1:
time: 730 us; the launch traced here: 729 us
  waiting for transfers between devices  474 us (65%)
  blocking collectives  188 us (26%)
  other arithmetic  21.5 us (3%)
  local copies, waits for them, and re-layouts  17.5 us (2%)
  between operations  13.9 us (2%)
  matrix products  13.7 us (2%)
    reduce_scatter x2, waiting for transfers between devices, body(): lax.psum_scatter(partial_value, 'dst', scatter_dimension=0, tiled=True)  430 us
    psum x2, blocking collectives, body(): scale_now = lax.psum(local_term, ('dst', 'src')) / S  160 us
    all_gather x2, waiting for transfers between devices, body(): lax.all_gather(forward[step_index], 'dst')  43.8 us
    all_gather x2, blocking collectives, body(): columns = lax.all_gather(message[:, :, None, :], 'src', axis=2, tiled=True)  28.5 us
    scatter-add x2, other arithmetic, body(): jax.ops.segment_sum(products, row_local, num_segments=total_rows)  16.1 us
  transfers between devices with their start and end apart: 4, of which 3 were waited for; matrix products, arithmetic and copies ran while one was open for 3% of the time, Pallas kernels for 0%

profile of v1, /device:TPU:1, one launch (start us, length us, event | category | flops | bytes accessed | tf_op | source)
XLA Modules:
  0.0 728.8 jit_solution(5440016924613923832)
XLA Ops:
  9.7 15.9 %all_gather.13 = bf16[32,4,8,128]{3,0,1,2:T(8,128)(2,1)S(1)} all-gather(bf16[32,4,1,128]{3,0,1,2:T(8,128)(2,1)S(1)} %fusion.24), channel_id=1, replica_groups=mesh['dst'=32,'src'=8] {'src'}, dimensions={2}, use_global_device_ids=true | all-gather | bytes 294912 | tf_op jit(solution)/shard_map/all_gather | solution.py:28
  25.9 1.4 gather_fusion.1
  27.3 2.3 convolution_multiply_fusion.1
  29.6 1.6 broadcast.28.clone
  31.2 8.0 %scatter_fusion = f32[128,32,128]{2,1,0:T(8,128)} fusion(f32[128,32,128]{2,1,0:T(8,128)} %broadcast.28.clone, s32[64]{0:T(128)S(1)} %get-tuple-element.28, f32[64,32,128]{2,1,0:T(8,128)S(1)} %convolution_multiply_fusion.1), kind=kCustom, calls=%fused_computation.6 | custom fusion | flops 262144 | bytes 3145984 | tf_op jit(solution)/shard_map/scatter-add | solution.py:38
  40.8 213.9 %reduce-scatter.3.cloned.1.call-done = f32[4,32,128]{2,1,0:T(8,128)} async-done(((f32[128,32,128]{2,1,0:T(8,128)}), f32[4,32,128]{2,1,0:T(8,128)}) %reduce-scatter.3.cloned.1.call-update) | async-done | bytes 65552 | tf_op jit(solution)/shard_map/reduce_scatter | solution.py:39
  254.7 1.0 multiply_reduce_fusion.1
  255.7 79.9 %psum.14 = f32[32]{0:T(128)S(1)} all-reduce(f32[32]{0:T(128)S(1)} %multiply_reduce_fusion.1), channel_id=1, replica_groups=mesh['dst'=32,'src'=8] {'dst','src'}, use_global_device_ids=true, to_apply=%region_2.5 | all-reduce | flops 32 | bytes 256 | tf_op jit(solution)/shard_map/psum | solution.py:44
  335.6 0.9 fusion.23
  336.5 12.6 %all-gather = bf16[32,4,1024]{2,0,1:T(8,128)(2,1)S(1)} all-gather(bf16[32,4,128]{2,0,1:T(8,128)(2,1)S(1)} %fusion.23), channel_id=2, replica_groups=mesh['dst'=32,'src'=8] {'src'}, dimensions={2}, use_global_device_ids=true | all-gather | bytes 294912 | tf_op jit(solution)/shard_map/all_gather | solution.py:28
  350.1 1.4 gather_fusion.4
  351.6 2.3 convolution_multiply_fusion
  353.8 1.6 broadcast.28
  355.4 8.0 %scatter_fusion.1 = f32[128,32,128]{2,1,0:T(8,128)} fusion(f32[128,32,128]{2,1,0:T(8,128)} %broadcast.28, s32[64]{0:T(128)S(1)} %copy-done.6, f32[64,32,128]{2,1,0:T(8,128)S(1)} %convolution_multiply_fusion), kind=kCustom, calls=%fused_computation.7 | custom fusion | flops 262144 | bytes 3145984 | tf_op jit(solution)/shard_map/scatter-add | solution.py:38
  363.6 1.9 gather_fusion.3
  365.5 43.8 %all-gather.4.cloned.1.call-done = bf16[32,32,4,1,128]{4,1,3,2,0:T(8,128)(2,1)} async-done(((bf16[1,32,4,1,128]{4,1,3,2,0:T(8,128)(2,1)}), bf16[32,32,4,1,128]{4,1,3,2,0:T(8,128)(2,1)}) %all-gather.4.cloned.1.call-update) | async-done | bytes 1048592 | tf_op jit(solution)/shard_map/all_gather | solution.py:30
  409.3 2.6 gather_fusion
  412.0 1.4 gather_fusion.2
  413.5 216.1 %reduce-scatter.5.cloned.1.call-done = f32[4,32,128]{2,1,0:T(8,128)} async-done(((f32[128,32,128]{2,1,0:T(8,128)}), f32[4,32,128]{2,1,0:T(8,128)}) %reduce-scatter.5.cloned.1.call-update) | async-done | bytes 65552 | tf_op jit(solution)/shard_map/reduce_scatter | solution.py:39
  629.6 1.0 multiply_reduce_fusion
  630.6 4.1 fusion.3
  634.7 79.6 %psum.15 = f32[32]{0:T(128)S(1)} all-reduce(f32[32]{0:T(128)S(1)} %multiply_reduce_fusion), channel_id=1, replica_groups=mesh['dst'=32,'src'=8] {'dst','src'}, use_global_device_ids=true, to_apply=%region_5.8 | all-reduce | flops 32 | bytes 256 | tf_op jit(solution)/shard_map/psum | solution.py:44
  715.2 1.4 gather_fusion.5
  717.2 5.0 multiply_convert_fusion
  (44 shorter events, 7.0 us)
Async XLA Ops:
  7.2 20.2 %copy-start = (bf16[64,128,128]{2,1,0:T(8,128)(2,1)S(1)}, bf16[64,128,128]{2,1,0:T(8,128)(2,1)}, u32[]{:S(2)}) copy-start(bf16[64,128,128]{2,1,0:T(8,128)(2,1)} %param.10) | copy-start | bytes 6291460
  7.2 247.6 %reduce-scatter.3.cloned.1.call-start = ((), (), s32[]{:S(2)}) async-start(), calls=%async_computation.3 | async-start | bytes 2162688 | tf_op jit(solution)/shard_map/reduce_scatter | solution.py:39
  8.1 23.1 %copy-start.5 = (s32[64]{0:T(128)}, s32[64]{0:T(128)S(1)}, u32[]{:S(2)}) copy-start(s32[64]{0:T(128)S(1)} %get-tuple-element.28) | copy-start | bytes 772
  31.2 8.1 %copy-start.4 = (bf16[2,32,4,1,128]{4,2,3,1,0:T(4,128)(2,1)S(1)}, bf16[2,32,4,1,128]{4,2,3,1,0:T(4,128)(2,1)}, u32[]{:S(2)}) copy-start(bf16[2,32,4,1,128]{4,2,3,1,0:T(4,128)(2,1)} %param.15) | copy-start | bytes 196612
  39.3 324.3 %all-gather.6.cloned.1.call-start = ((), (), s32[]{:S(2)}) async-start(), calls=%async_computation.4 | async-start | bytes 1081344 | tf_op jit(solution)/shard_map/all_gather | solution.py:30
  40.0 369.3 %all-gather.4.cloned.1.call-start = ((), (), s32[]{:S(2)}) async-start(), calls=%async_computation.2 | async-start | bytes 1081344 | tf_op jit(solution)/shard_map/all_gather | solution.py:30
  40.8 588.9 %reduce-scatter.5.cloned.1.call-start = ((), (), s32[]{:S(2)}) async-start(), calls=%async_computation.5 | async-start | bytes 2162688 | tf_op jit(solution)/shard_map/reduce_scatter | solution.py:39
  349.4 0.7 copy-start.1
  351.6 3.9 copy-start.6
  630.6 83.8 %copy-start.2 = (bf16[32,32,128]{2,1,0:T(8,128)(2,1)S(1)}, bf16[32,32,128]{2,1,0:T(8,128)(2,1)}, u32[]{:S(2)}) copy-start(bf16[32,32,128]{2,1,0:T(8,128)(2,1)} %copy-done.1) | copy-start | bytes 786436
  630.6 83.9 %copy-start.3 = (f32[4,32,128]{2,1,0:T(8,128)S(1)}, f32[4,32,128]{2,1,0:T(8,128)}, u32[]{:S(2)}) copy-start(f32[4,32,128]{2,1,0:T(8,128)} %reduce-scatter.5.cloned.1.call-done) | copy-start | bytes 196612
Sparse Core Ops, SparseCore 0:
  39.4 215.2 reduce-scatter.2
  257.3 74.8 all-gather.5
  335.4 73.8 all-gather.3
  413.5 216.0 reduce-scatter.4
